TPU v7x, 32 devices: a whole 2x2x4 slice. The times are simulated.
32 devices in a mesh: seq: 4 (over y, core), tp: 8 (over z, x).
Axes of the slice: x: 2, y: 2, z: 4, core: 2. Of those that a mesh axis runs over, the one named last changes fastest.
Arguments:
- tokens: bfloat16 [2048, 8192], P('seq', 'tp'), may hold values from -6 to 6
- w_query: bfloat16 [8192, 6144], P(None, 'tp'), may hold values from -0.0625 to 0.0625
- w_key: bfloat16 [8192, 6144], P(None, 'tp'), may hold values from -0.0625 to 0.0625
- w_value: bfloat16 [8192, 6144], P(None, 'tp'), may hold values from -0.0625 to 0.0625
- w_out: bfloat16 [6144, 8192], P('tp'), may hold values from -0.109375 to 0.109375
- carry: float32 [48, 128, 128], P('tp'), may hold values from -40 to 40
Outputs:
- mixed: bfloat16 [2048, 8192], P('seq', 'tp')
All inputs are finite; a program needn't handle non-finite values.
Results may differ from a plain program's by a relative error of at most 0.0066.
Values may be sent and summed in bfloat16 or wider, within the bound.
No kernel may reach another device: no remote copies, remote signals or barrier semaphores. Data moves between devices by JAX's collectives and lax.ppermute only.
A program may use at most 192 MiB of HBM per device.

v0:
```python
import jax
import jax.numpy as jnp
from jax import lax
from jax.sharding import PartitionSpec as P

EPSILON = 1e-05


def entering(array, axis, combine, identity):
    count, place = (lax.axis_size(axis), lax.axis_index(axis))
    everything = lax.all_gather(array, axis)
    start = jnp.broadcast_to(jnp.asarray(identity, array.dtype), array.shape)

    def turn(k, before):
        reached = k < place
        new = combine(before, everything[k])
        return jnp.where(reached, new, before)

    return lax.fori_loop(0, count, turn, start)


def combine_states(earlier, latter_part):
    return earlier + latter_part


def local(tokens, w_query, w_key, w_value, w_out, carry):
    row_count = tokens.shape[0]
    head_count = carry.shape[0]
    head_size = carry.shape[1]
    proj_width = w_query.shape[1]
    segment = lax.all_gather(tokens, "tp", axis=1, tiled=True)
    query_sum = jnp.dot(segment, w_query, preferred_element_type=jnp.float32)
    key_sum = jnp.dot(segment, w_key, preferred_element_type=jnp.float32)
    value_sum = jnp.dot(segment, w_value, preferred_element_type=jnp.float32)
    query = query_sum.astype(jnp.bfloat16).reshape(row_count, head_count, head_size)
    keys_local = key_sum.astype(jnp.bfloat16).reshape(row_count, head_count, head_size)
    values_local = value_sum.astype(jnp.bfloat16).reshape(row_count, head_count, head_size)
    local_state = jnp.einsum(
        "thd,the->hde", keys_local, values_local, preferred_element_type=jnp.float32
    )
    earlier_sum = entering(local_state, "seq", combine_states, jnp.zeros_like(local_state))
    prior = carry + earlier_sum
    across = jnp.einsum(
        "thd,hde->the", query.astype(jnp.float32), prior, precision=lax.Precision.HIGHEST
    )
    causal = lax.broadcasted_iota(jnp.int32, (row_count, row_count), 0) >= lax.broadcasted_iota(
        jnp.int32, (row_count, row_count), 1
    )
    scores = jnp.einsum("thd,shd->hts", query, keys_local, preferred_element_type=jnp.float32)
    scores = jnp.where(causal[None], scores, 0.0).astype(jnp.bfloat16)
    within = jnp.einsum("hts,she->the", scores, values_local, preferred_element_type=jnp.float32)
    total = across + within
    normed = total * lax.rsqrt(jnp.mean(total * total, axis=-1, keepdims=True) + EPSILON)
    attended = normed.astype(jnp.bfloat16).reshape(row_count, proj_width)
    summed = lax.psum_scatter(
        lax.dot_general(
            w_out, attended, (((0,), (1,)), ((), ())), preferred_element_type=jnp.float32
        ),
        "tp",
        scatter_dimension=0,
        tiled=True,
    )
    return summed.T.astype(jnp.bfloat16)


def solution(mesh):
    placed = (
        P("seq", "tp"),
        P(None, "tp"),
        P(None, "tp"),
        P(None, "tp"),
        P("tp", None),
        P("tp", None, None),
    )
    return jax.shard_map(
        local, mesh=mesh, in_specs=placed, out_specs=P("seq", "tp"), check_vma=False
    )
```

profile of v0, /device:TPU:0, one launch (start us, length us, event | category | flops | bytes accessed | tf_op | source)
XLA Modules:
  0.0 496.5 jit_solution(3666014107982523729)
XLA Ops:
  6.5 0.7 all-gather.4.cloned.1.call-update
  7.3 0.0 all-gather.6.cloned.1.call-start
  7.3 129.9 %all-gather.4.cloned.1.call-done = bf16[512,8192]{1,0:T(8,128)(2,1)} async-done(((bf16[512,1024]{1,0:T(8,128)(2,1)}), bf16[512,8192]{1,0:T(8,128)(2,1)}) %all-gather.4.cloned.1.call-update) | async-done | bytes 8388624 | tf_op jit(solution)/shard_map/all_gather | solution.py:31
  137.2 12.7 %convolution_convert_fusion.2 = bf16[512,768]{1,0:T(8,128)(2,1)S(1)} fusion(bf16[512,8192]{1,0:T(8,128)(2,1)} %all-gather.4.cloned.1.call-done, bf16[8192,768]{1,0:T(8,128)(2,1)} %param.10), kind=kOutput, calls=%fused_computation.14 | convolution fusion | flops 6442844160 | bytes 21757952 | tf_op jit(solution)/shard_map/dot_general | solution.py:33
  149.9 0.3 copy.18
  150.2 12.7 %convolution_convert_fusion.1 = bf16[512,768]{1,0:T(8,128)(2,1)S(1)} fusion(bf16[512,8192]{1,0:T(8,128)(2,1)} %all-gather.4.cloned.1.call-done, bf16[8192,768]{1,0:T(8,128)(2,1)} %param.11), kind=kOutput, calls=%fused_computation.13 | convolution fusion | flops 6442844160 | bytes 21757952 | tf_op jit(solution)/shard_map/dot_general | solution.py:34
  162.9 0.3 copy.19
  163.2 1.1 fusion.9
  164.3 0.0 all-gather.6.cloned.1.call-update
  164.3 0.2 reduce-scatter.2.cloned.1.call-start
  164.6 0.8 iota_compare_fusion
  165.3 13.2 %convolution_convert_fusion = bf16[512,768]{1,0:T(8,128)(2,1)S(1)} fusion(bf16[512,8192]{1,0:T(8,128)(2,1)} %all-gather.4.cloned.1.call-done, bf16[8192,768]{1,0:T(8,128)(2,1)} %param.9), kind=kOutput, calls=%fused_computation.12 | convolution fusion | flops 6442844160 | bytes 21757952 | tf_op jit(solution)/shard_map/dot_general | solution.py:32
  178.6 0.3 copy.21
  178.9 4.2 fusion
  183.1 4.6 while.14
  183.1 1.1 add_select_fusion.2
  184.2 1.1 add_select_fusion.2
  185.4 1.1 add_select_fusion.2
  186.5 1.1 add_select_fusion.2
  187.7 2.4 fusion.5
  190.1 0.2 fusion.6
  190.3 14.8 %convolution_bitcast_fusion = f32[8192,512]{0,1:T(8,128)} fusion(bf16[512,768]{0,1:T(8,128)(2,1)S(1)} %bitcast.34, bf16[768,8192]{1,0:T(8,128)(2,1)} %param.12), kind=kOutput, calls=%fused_computation.1 | convolution fusion | flops 6442450944 | bytes 30146560 | tf_op jit(solution)/shard_map/dot_general | solution.py:56
  205.1 282.1 %reduce-scatter.2.cloned.1.call-done = f32[1024,512]{0,1:T(8,128)} async-done(((f32[8192,512]{0,1:T(8,128)}), f32[1024,512]{0,1:T(8,128)}) %reduce-scatter.2.cloned.1.call-update) | async-done | bytes 2097168 | tf_op jit(solution)/shard_map/reduce_scatter | solution.py:55
  487.2 2.7 convert_bitcast_fusion
  (7 shorter events, 0.0 us)
Async XLA Ops:
  6.5 130.7 %all-gather.4.cloned.1.call-start = ((), (), s32[]{:S(2)}) async-start(), calls=%async_computation.1 | async-start | bytes 9437184 | tf_op jit(solution)/shard_map/all_gather | solution.py:31
  7.3 175.8 %all-gather.6.cloned.1.call-start = ((), (), s32[]{:S(2)}) async-start(), calls=%async_computation.3 | async-start | bytes 1966080 | tf_op jit(solution)/shard_map/all_gather | solution.py:11
  164.3 322.9 %reduce-scatter.2.cloned.1.call-start = ((), (), s32[]{:S(2)}) async-start(), calls=%async_computation.2 | async-start | bytes 18874368 | tf_op jit(solution)/shard_map/reduce_scatter | solution.py:55
  178.9 8.8 %copy-start = (f32[6,128,128]{2,1,0:T(8,128)S(1)}, f32[6,128,128]{2,1,0:T(8,128)}, u32[]{:S(2)}) copy-start(f32[6,128,128]{2,1,0:T(8,128)} %param.13) | copy-start | bytes 1179652
Sparse Core Ops, SparseCore 0:
  9.5 127.5 all-gather.3
  164.4 17.8 all-gather.5
  205.2 281.9 reduce-scatter.1
where the time goes:
time: 497 us; the launch traced here: 496 us
  waiting for transfers between devices  413 us (83%)
  matrix products  61.1 us (12%)
  between operations  13.2 us (3%)
  other arithmetic  8.24 us (2%)
    reduce_scatter x1, waiting for transfers between devices, local(): lax.psum_scatter(lax.dot_general(w_out, attended, (((0,), (1,)), ((), ())...  282 us
    all_gather x1, waiting for transfers between devices, local(): segment = lax.all_gather(tokens, 'tp', axis=1, tiled=True)  130 us
    dot_general x1, matrix products, local(): lax.dot_general(w_out, attended, (((0,), (1,)), ((), ())), preferred_elem...  14.8 us
    dot_general x1, matrix products, local(): query_sum = jnp.dot(segment, w_query, preferred_element_type=jnp.float32)  13.2 us
    dot_general x1, matrix products, local(): key_sum = jnp.dot(segment, w_key, preferred_element_type=jnp.float32)  12.7 us
    dot_general x1, matrix products, local(): value_sum = jnp.dot(segment, w_value, preferred_element_type=jnp.float32)  12.7 us
  transfers between devices with their start and end apart: 3, of which 2 were waited for; matrix products, arithmetic and copies ran while one was open for 4% of the time, Pallas kernels for 0%

commit v1 on v0

--- a/solution.py
+++ b/solution.py
@@ -4,6 +4,24 @@
 from jax.sharding import PartitionSpec as P
 
 EPSILON = 1e-05
+
+
+def joined_along(parts, dim):
+    dims = list(parts.shape[1:])
+    dims[dim] *= parts.shape[0]
+    return jnp.moveaxis(parts, 0, dim).reshape(dims)
+
+
+def grow_blocks(array, axis):
+    length = lax.axis_size(axis)
+    blocks = array[None]
+    for level in range(length.bit_length() - 1):
+        bit = 1 << level
+        other = lax.ppermute(blocks, axis, [(i, i ^ bit) for i in range(length)])
+        both = jnp.stack([blocks, other])
+        upper = lax.axis_index(axis) >> level & 1
+        blocks = jnp.where(upper == 0, both, both[::-1]).reshape(-1, *array.shape)
+    return blocks
 
 
 def entering(array, axis, combine, identity):
@@ -28,7 +46,7 @@
     head_count = carry.shape[0]
     head_size = carry.shape[1]
     proj_width = w_query.shape[1]
-    segment = lax.all_gather(tokens, "tp", axis=1, tiled=True)
+    segment = joined_along(grow_blocks(tokens, "tp"), 1)
     query_sum = jnp.dot(segment, w_query, preferred_element_type=jnp.float32)
     key_sum = jnp.dot(segment, w_key, preferred_element_type=jnp.float32)
     value_sum = jnp.dot(segment, w_value, preferred_element_type=jnp.float32)

time: 497 us -> 656 us (1.32)
  waiting for transfers between devices: 413 us -> 527 us
  other arithmetic: 8.24 us -> 36 us
  local copies, waits for them, and re-layouts: 0.84 us -> 13.3 us
  starting transfers between devices: 0.26 us -> 7.33 us
    ppermute x0 -> x3, waiting for transfers between devices: none -> 242 us  [grow_blocks(): other = lax.ppermute(blocks, axis, [(i, i ^ bit) for i in range(length)])]
    all_gather x1 -> x0, waiting for transfers between devices: 130 us -> none  [local(): segment = lax.all_gather(tokens, 'tp', axis=1, tiled=True)]
    select_n x0 -> x2, other arithmetic: none -> 14.7 us  [grow_blocks(): blocks = jnp.where(upper == 0, both, both[::-1]).reshape(-1, *array.shape)]
    another operation x0 -> x4, other arithmetic: none -> 13 us  [grow_blocks(): both = jnp.stack([blocks, other])]
    ppermute x0 -> x3, starting transfers between devices: none -> 7.29 us  [grow_blocks(): other = lax.ppermute(blocks, axis, [(i, i ^ bit) for i in range(length)])]
  transfers between devices with their start and end apart: 3 -> 5, of which waited for: 2 -> 5; matrix products, arithmetic and copies ran while one was open for 4% -> 4% of each run, Pallas kernels for 0% -> 0%
where the time goes in v1:
time: 656 us; the launch traced here: 655 us
  waiting for transfers between devices  527 us (80%)
  matrix products  58 us (9%)
  other arithmetic  36 us (5%)
  between operations  13.5 us (2%)
  local copies, waits for them, and re-layouts  13.3 us (2%)
  starting transfers between devices  7.33 us (1%)
    reduce_scatter x1, waiting for transfers between devices, local(): lax.psum_scatter(lax.dot_general(w_out, attended, (((0,), (1,)), ((), ())...  283 us
    ppermute x3, waiting for transfers between devices, grow_blocks(): other = lax.ppermute(blocks, axis, [(i, i ^ bit) for i in range(length)])  242 us
    dot_general x1, matrix products, local(): lax.dot_general(w_out, attended, (((0,), (1,)), ((), ())), preferred_elem...  14.8 us
    select_n x2, other arithmetic, grow_blocks(): blocks = jnp.where(upper == 0, both, both[::-1]).reshape(-1, *array.shape)  14.7 us
  transfers between devices with their start and end apart: 5, of which 5 were waited for; matrix products, arithmetic and copies ran while one was open for 4% of the time, Pallas kernels for 0%

profile of v1, /device:TPU:0, one launch (start us, length us, event | category | flops | bytes accessed | tf_op | source)
XLA Modules:
  0.0 655.5 jit_solution(2264821831291554191)
XLA Ops:
  6.5 2.9 collective-permute-start
  9.5 23.4 %collective-permute-done = bf16[1,512,1024]{2,1,0:T(8,128)(2,1)S(1)} collective-permute-done((bf16[1,512,1024]{2,1,0:T(8,128)(2,1)}, bf16[1,512,1024]{2,1,0:T(8,128)(2,1)S(1)}, u32[]{:S(2)}, u32[]{:S(2)}) %collective-permute-start) | collective-permute-done | bytes 1048608 | tf_op jit(solution)/shard_map/ppermute | solution.py:20
  32.8 1.4 pad_maximum_fusion.2
  34.3 2.2 fusion.6
  36.4 1.8 collective-permute-start.1
  38.3 45.3 %collective-permute-done.1 = bf16[2,512,1024]{2,1,0:T(8,128)(2,1)} collective-permute-done((bf16[2,512,1024]{2,1,0:T(8,128)(2,1)}, bf16[2,512,1024]{2,1,0:T(8,128)(2,1)}, u32[]{:S(2)}, u32[]{:S(2)}) %collective-permute-start.1) | collective-permute-done | bytes 2097184 | tf_op jit(solution)/shard_map/ppermute | solution.py:20
  83.6 2.0 pad_maximum_fusion.1
  85.6 3.2 reverse_select_fusion.1
  88.7 6.2 copy.20
  95.0 2.5 collective-permute-start.2
  97.5 6.3 copy.21
  103.8 173.2 %collective-permute-done.2 = bf16[4,512,1024]{1,2,0:T(8,128)(2,1)} collective-permute-done((bf16[4,512,1024]{1,2,0:T(8,128)(2,1)}, bf16[4,512,1024]{1,2,0:T(8,128)(2,1)}, u32[]{:S(2)}, u32[]{:S(2)}) %collective-permute-start.2) | collective-permute-done | bytes 4194336 | tf_op jit(solution)/shard_map/ppermute | solution.py:20
  276.9 7.5 %pad_maximum_fusion = bf16[2,4,512,1024]{2,3,1,0:T(8,128)(2,1)} fusion(bf16[1,4,512,1024]{2,3,1,0:T(8,128)(2,1)} %bitcast.8, bf16[1,4,512,1024]{2,3,1,0:T(8,128)(2,1)} %copy.21), kind=kLoop, calls=%fused_computation.3 | loop fusion | flops 4194304 | bytes 16777216 | tf_op jit(solution)/shard_map/stack | solution.py:21
  284.4 11.5 %reverse_select_fusion = bf16[2,4,512,1024]{2,3,1,0:T(8,128)(2,1)} fusion(bf16[2,4,512,1024]{2,3,1,0:T(8,128)(2,1)} %pad_maximum_fusion, pred[]{:T(512)S(6)} %eq.9), kind=kLoop, calls=%fused_computation.2 | loop fusion | flops 4194304 | bytes 16777216 | tf_op jit(solution)/shard_map/jit(_where)/select_n | solution.py:23
  295.9 12.9 %convolution_convert_fusion.1 = bf16[512,768]{1,0:T(8,128)(2,1)S(1)} fusion(bf16[512,8192]{0,1:T(8,128)(2,1)} %bitcast.52, bf16[8192,768]{1,0:T(8,128)(2,1)} %param.11), kind=kOutput, calls=%fused_computation.21 | convolution fusion | flops 6442844160 | bytes 21757952 | tf_op jit(solution)/shard_map/dot_general | solution.py:52
  308.8 9.9 %convolution_convert_fusion.2 = bf16[512,768]{1,0:T(8,128)(2,1)S(1)} fusion(bf16[512,8192]{0,1:T(8,128)(2,1)S(1)} %bitcast.54, bf16[8192,768]{1,0:T(8,128)(2,1)} %param.10), kind=kOutput, calls=%fused_computation.22 | convolution fusion | flops 6442844160 | bytes 21757952 | tf_op jit(solution)/shard_map/dot_general | solution.py:51
  321.3 12.8 %convolution_convert_fusion = bf16[512,768]{1,0:T(8,128)(2,1)S(1)} fusion(bf16[512,8192]{0,1:T(8,128)(2,1)} %bitcast.53, bf16[8192,768]{1,0:T(8,128)(2,1)} %param.9), kind=kOutput, calls=%fused_computation.20 | convolution fusion | flops 6442844160 | bytes 21757952 | tf_op jit(solution)/shard_map/dot_general | solution.py:50
  334.4 4.1 fusion
  338.5 2.6 all-gather.3.cloned.1.call-done
  341.0 4.6 while.14
  345.7 2.4 fusion.7
  348.3 14.8 %convolution_bitcast_fusion = f32[8192,512]{0,1:T(8,128)} fusion(bf16[512,768]{0,1:T(8,128)(2,1)S(1)} %bitcast.55, bf16[768,8192]{1,0:T(8,128)(2,1)} %param.12), kind=kOutput, calls=%fused_computation.1 | convolution fusion | flops 6442450944 | bytes 30146560 | tf_op jit(solution)/shard_map/dot_general | solution.py:74
  363.1 282.8 %reduce-scatter.2.cloned.1.call-done = f32[1024,512]{0,1:T(8,128)} async-done(((f32[8192,512]{0,1:T(8,128)}), f32[1024,512]{0,1:T(8,128)}) %reduce-scatter.2.cloned.1.call-update) | async-done | bytes 2097168 | tf_op jit(solution)/shard_map/reduce_scatter | solution.py:73
  645.9 2.7 convert_bitcast_fusion
  (20 shorter events, 7.6 us)
Async XLA Ops:
  6.5 334.5 %all-gather.3.cloned.1.call-start = ((), (), s32[]{:S(2)}) async-start(), calls=%async_computation.2 | async-start | bytes 1966080 | tf_op jit(solution)/shard_map/all_gather | solution.py:29
  6.5 26.3 %collective-permute-start = (bf16[1,512,1024]{2,1,0:T(8,128)(2,1)}, bf16[1,512,1024]{2,1,0:T(8,128)(2,1)S(1)}, u32[]{:S(2)}, u32[]{:S(2)}) collective-permute-start(bf16[1,512,1024]{2,1,0:T(8,128)(2,1)} %bitcast.63), channel_id=1, source_target_pairs={{0,1},{1,0},{2,3},{3,2},{4,5},{5,4},{6,7},{7,6},{8,9},{9,8},{10,11... | collective-permute-start | bytes 3145736 | tf_op jit(solution)/shard_map/ppermute | solution.py:20
  36.4 47.1 %collective-permute-start.1 = (bf16[2,512,1024]{2,1,0:T(8,128)(2,1)}, bf16[2,512,1024]{2,1,0:T(8,128)(2,1)}, u32[]{:S(2)}, u32[]{:S(2)}) collective-permute-start(bf16[2,512,1024]{2,1,0:T(8,128)(2,1)} %get-tuple-element.109), channel_id=1, source_target_pairs={{0,2},{1,3},{2,0},{3,1},{4,6},{5,7},{6,4},{7,5},{8,10},{9,11},{10,... | collective-permute-start | bytes 6291464 | tf_op jit(solution)/shard_map/ppermute | solution.py:20
  95.0 181.9 %collective-permute-start.2 = (bf16[4,512,1024]{1,2,0:T(8,128)(2,1)}, bf16[4,512,1024]{1,2,0:T(8,128)(2,1)}, u32[]{:S(2)}, u32[]{:S(2)}) collective-permute-start(bf16[4,512,1024]{1,2,0:T(8,128)(2,1)} %copy.20), channel_id=1, source_target_pairs={{0,4},{1,5},{2,6},{3,7},{4,0},{5,1},{6,2},{7,3},{8,12},{9,13},{10,... | collective-permute-start | bytes 12582920 | tf_op jit(solution)/shard_map/ppermute | solution.py:20
  295.9 12.9 %copy-start = (bf16[2,4,512,1024]{2,3,1,0:T(8,128)(2,1)S(1)}, bf16[2,4,512,1024]{2,3,1,0:T(8,128)(2,1)}, u32[]{:S(2)}) copy-start(bf16[2,4,512,1024]{2,3,1,0:T(8,128)(2,1)} %reverse_select_fusion) | copy-start | bytes 25165828
  320.5 325.4 %reduce-scatter.2.cloned.1.call-start = ((), (), s32[]{:S(2)}) async-start(), calls=%async_computation.1 | async-start | bytes 18874368 | tf_op jit(solution)/shard_map/reduce_scatter | solution.py:73
  338.5 7.2 %copy-start.1 = (f32[6,128,128]{2,1,0:T(8,128)S(1)}, f32[6,128,128]{2,1,0:T(8,128)}, u32[]{:S(2)}) copy-start(f32[6,128,128]{2,1,0:T(8,128)} %param.13) | copy-start | bytes 1179652
Sparse Core Ops, SparseCore 0:
  320.6 20.4 all-gather.2
  363.2 282.6 reduce-scatter.1
